TPU v7x, 32 devices: a whole 2x2x4 slice. The times are simulated.
32 devices in a mesh: group: 4 (over z), expert: 8 (over y, x, core).
Axes of the slice: x: 2, y: 2, z: 4, core: 2. Of those that a mesh axis runs over, the one named last changes fastest.
Arguments:
- group_logits: float32 [4096, 4], P(('group', 'expert')), may hold values from -6 to 6
- expert_logits: float32 [4096, 32], P(('group', 'expert')), may hold values from -6 to 6
- expert_ids: int32 [4096, 2], P(('group', 'expert')), may hold values from 0 to 31, all different within a row; in each aligned block of 128 rows (0 to 127, 128 to 255, ...) at most 16 rows name the same one
- cotangent: bfloat16 [4096, 3584], P(('group', 'expert')), may hold values from -6 to 6
- hidden_saved: bfloat16 [32, 512, 1024], P(('group', 'expert')), may hold values from -0.1875 to 0.1875
- w_down: bfloat16 [32, 1024, 3584], P(('group', 'expert')), may hold values from -0.1875 to 0.1875
Outputs:
- hidden_grad: bfloat16 [32, 512, 1024], P(('group', 'expert'))
- d_group_logits: float32 [4096, 4], P(('group', 'expert'))
- d_expert_logits: float32 [4096, 32], P(('group', 'expert'))
Inputs may be any that keep to these rules, and one draw needn't show every extreme that they name: `expert_ids`: within the 128 tokens of one device no expert is named by more than 16 choices, a bound that some block reaches; the 2 experts of a token differ.
All inputs are finite; a program needn't handle non-finite values.
Results may differ from a plain program's by a relative error of at most 0.0045.
Values may be sent and summed in bfloat16 or wider, within the bound.
No kernel may reach another device: no remote copies, remote signals or barrier semaphores. Data moves between devices by JAX's collectives and lax.ppermute only.
A program may use at most 64 MiB of HBM per device.

v0:
```python
from functools import partial
import jax
import jax.numpy as jnp
from jax import lax
from jax.sharding import PartitionSpec as P

ITERS = 5
SOFTCAP = 4.0


def capped(logits):
    return jnp.exp(SOFTCAP * jnp.tanh(logits / SOFTCAP))


def squashing(logits):
    bounded = jnp.tanh(logits / SOFTCAP)
    return 1.0 - bounded * bounded


def balance_level(level_in, target, column_sum):
    scaled = level_in * (target / column_sum)
    return (scaled, jnp.sum(scaled, -1, keepdims=True))


def adjoint_local(out_grad, level_in, target, column_sum):
    scaled, row_total = balance_level(level_in, target, column_sum)
    level_out = scaled / row_total
    scaled_grad = (out_grad - jnp.sum(out_grad * level_out, -1, keepdims=True)) / row_total
    return (scaled_grad, jnp.sum(scaled_grad * level_in, 0))


def adjoint_finish(scaled_grad, inner, target, column_sum):
    return target / column_sum * (scaled_grad - inner / column_sum)


def balance_step(targets, current, unused):
    target_group, target_expert = targets
    group_in, expert_in = current
    group_cols, expert_cols = lax.psum(
        (jnp.sum(group_in, 0), jnp.sum(expert_in, 0)), ("group", "expert")
    )
    scaled_g, rowsum_g = balance_level(group_in, target_group, group_cols)
    scaled_e, rowsum_e = balance_level(expert_in, target_expert, expert_cols)
    return (
        (scaled_g / rowsum_g, scaled_e / rowsum_e),
        (group_in, expert_in, group_cols, expert_cols),
    )


def adjoint_step(targets, carried, stored_step):
    target_group, target_expert = targets
    grad_g, grad_e = carried
    group_in, expert_in, group_cols, expert_cols = stored_step
    scaled_g, inner_g = adjoint_local(grad_g, group_in, target_group, group_cols)
    scaled_e, inner_e = adjoint_local(grad_e, expert_in, target_expert, expert_cols)
    inner_g, inner_e = lax.psum((inner_g, inner_e), ("group", "expert"))
    next_g = adjoint_finish(scaled_g, inner_g, target_group, group_cols)
    next_e = adjoint_finish(scaled_e, inner_e, target_expert, expert_cols)
    return ((next_g, next_e), None)


def deliver(payload):
    halfway = (
        lax.all_to_all(payload[0], "expert", split_axis=1, concat_axis=1, tiled=True),
        lax.all_to_all(payload[1], "expert", split_axis=1, concat_axis=1, tiled=True),
    )
    return (
        lax.all_to_all(halfway[0], "group", split_axis=0, concat_axis=0, tiled=True),
        lax.all_to_all(halfway[1], "group", split_axis=0, concat_axis=0, tiled=True),
    )


def per_device(group_logits, expert_logits, expert_ids, cotangent, hidden_saved, w_down):
    groups = lax.axis_size("group")
    per_group = lax.axis_size("expert")
    experts = groups * per_group
    tokens_here = cotangent.shape[0]
    top_count = expert_ids.shape[1]
    model_width = cotangent.shape[1]
    capacity = hidden_saved.shape[1] // experts
    targets = (float(tokens_here * per_group), float(tokens_here * groups))
    flat_ids = expert_ids.reshape(-1)
    picked = (flat_ids[:, None] == jnp.arange(experts, dtype=jnp.int32)[None, :]).astype(jnp.int32)
    positions = jnp.sum((jnp.cumsum(picked, 0) - picked) * picked, 1)
    slot_index = flat_ids * capacity + positions
    serial = jnp.arange(flat_ids.shape[0], dtype=jnp.int32)
    source_index = jnp.zeros((experts * capacity,), jnp.int32).at[slot_index].set(serial)
    filled = jnp.zeros((experts * capacity,), jnp.int32).at[slot_index].set(1)
    fetched = jnp.take(cotangent, source_index // top_count, axis=0)
    send_rows = jnp.where(filled[:, None] > 0, fetched, jnp.zeros_like(fetched))
    send_rows = send_rows.reshape(groups, per_group, capacity, model_width)
    group_of = expert_ids // per_group
    group_aff = capped(group_logits)
    expert_aff = capped(expert_logits).reshape(tokens_here, groups, per_group)
    (group_prob, expert_prob), stored = lax.scan(
        partial(balance_step, targets), (group_aff, expert_aff), None, length=ITERS
    )
    pick_group = jnp.take_along_axis(group_prob, group_of, 1)
    pick_expert = jnp.take_along_axis(expert_prob.reshape(tokens_here, experts), expert_ids, 1)
    pair_prob = pick_group * pick_expert
    total_prob = jnp.sum(pair_prob, 1, keepdims=True)
    gate_prob = pair_prob / total_prob
    gate_sent = (
        jnp.zeros((experts * capacity,), jnp.bfloat16)
        .at[slot_index]
        .set(gate_prob.astype(jnp.bfloat16).reshape(-1))
    )
    gate_sent = gate_sent.reshape(groups, per_group, capacity)
    routed = (
        group_aff,
        expert_aff,
        stored,
        pick_group,
        pick_expert,
        total_prob,
        gate_prob,
        gate_sent,
    )
    got_rows, got_gates = deliver((send_rows, routed[7]))
    group_aff, expert_aff, stored, pick_group, pick_expert, total_prob, gate_prob, unused_gates = (
        routed
    )
    weight = w_down[0]
    saved_hidden = hidden_saved[0]
    expert_rows = got_rows.reshape(-1, model_width)
    unscaled = lax.dot_general(
        expert_rows, weight, (((1,), (1,)), ((), ())), preferred_element_type=jnp.float32
    )
    slot_grad = jnp.sum(unscaled * saved_hidden.astype(jnp.float32), 1)
    grad_rows = (got_gates.reshape(-1, 1).astype(jnp.float32) * unscaled).astype(jnp.bfloat16)
    hidden_grad = grad_rows[None]
    answers = lax.all_to_all(
        lax.all_to_all(
            slot_grad.reshape(groups, per_group, capacity),
            "group",
            split_axis=0,
            concat_axis=0,
            tiled=True,
        ),
        "expert",
        split_axis=1,
        concat_axis=1,
        tiled=True,
    )
    gate_grad = answers.reshape(-1)[slot_index].reshape(tokens_here, top_count)
    pair_grad = (gate_grad - jnp.sum(gate_prob * gate_grad, 1, keepdims=True)) / total_prob
    group_pick = (
        group_of[:, :, None] == jnp.arange(groups, dtype=jnp.int32)[None, None, :]
    ).astype(jnp.float32)
    seed_group = jnp.sum(group_pick * (pair_grad * pick_expert)[:, :, None], 1)
    expert_pick = (
        expert_ids[:, :, None] == jnp.arange(experts, dtype=jnp.int32)[None, None, :]
    ).astype(jnp.float32)
    seed_expert = jnp.sum(expert_pick * (pair_grad * pick_group)[:, :, None], 1).reshape(
        tokens_here, groups, per_group
    )
    (grad_group, grad_expert), unused = lax.scan(
        partial(adjoint_step, targets), (seed_group, seed_expert), stored, reverse=True
    )
    d_group_logits = grad_group * group_aff * squashing(group_logits)
    d_expert_logits = (grad_expert * expert_aff).reshape(tokens_here, experts) * squashing(
        expert_logits
    )
    return (hidden_grad, d_group_logits, d_expert_logits)


def solution(mesh):
    in_specs = (
        P(("group", "expert"), None),
        P(("group", "expert"), None),
        P(("group", "expert"), None),
        P(("group", "expert"), None),
        P(("group", "expert"), None, None),
        P(("group", "expert"), None, None),
    )
    out_specs = (
        P(("group", "expert"), None, None),
        P(("group", "expert"), None),
        P(("group", "expert"), None),
    )
    return jax.shard_map(
        per_device, mesh=mesh, in_specs=in_specs, out_specs=out_specs, check_vma=False
    )
```

profile of v0, /device:TPU:0, one launch (start us, length us, event | category | flops | bytes accessed | tf_op | source)
XLA Modules:
  0.0 600.4 jit_solution(14312915412681843163)
XLA Ops:
  0.6 0.9 copy.101
  1.5 0.1 eq.55
  1.7 0.1 eq.51
  1.8 0.7 broadcast_multiply_fusion
  2.5 0.6 reduce-window.6
  3.1 0.2 slice_reduce_fusion
  3.4 0.1 mul.222
  3.7 1.4 scatter_custom_fusion.2
  5.2 1.4 scatter_custom_fusion.1
  6.8 4.2 gather_fusion
  10.9 3.6 fusion.16
  14.6 5.3 all-to-all-start.2
  20.1 0.1 reshape.221
  20.3 43.2 %all-to-all-done.2 = bf16[4,8,16,3584]{3,2,0,1:T(8,128)(2,1)} async-done(((bf16[4,8,16,3584]{3,2,0,1:T(8,128)(2,1)}), bf16[4,8,16,3584]{3,2,0,1:T(8,128)(2,1)}, u32[]{:S(2)}, u32[]{:S(2)}) %all-to-all-start.2) | async-done | bytes 3670048 | tf_op jit(solution)/shard_map/all_to_all | solution.py:64
  63.5 4.2 copy.114
  67.6 5.6 all-to-all-start.3
  73.2 264.1 %while.36 = (s32[]{:T(128)}, f32[128,4]{0,1:T(4,128)S(1)}, f32[128,4,8]{0,2,1:T(8,128)S(1)}, f32[5,128,4]{1,2,0:T(4,128)S(1)}, f32[5,128,4,8]{1,3,2,0:T(8,128)S(...) while((s32[]{:T(128)}, f32[128,4]{0,1:T(4,128)S(1)}, ...), condition=%wide.region_10.11_spmd, body=%wide.region_3.10_spmd.sunk | while | flops 15277 | bytes 133133 | solution.py:95
  73.4 100.2 %all-reduce.4 = (f32[4]{0:T(128)S(1)}, f32[4,8]{1,0:T(4,128)S(1)}) all-reduce(f32[4]{0:T(128)S(1)} %reduce_sum.212, f32[4,8]{1,0:T(4,128)S(1)} %reduce_sum.213), channel_id=1, replica_groups=mesh['group'=4,'expert'=8] {'group','expert'}, use_global_device_ids=true, to_apply=%region_5.5 | all-reduce | flops 36 | bytes 288 | tf_op jit(solution)/shard_map/while/body/eval_jaxpr/psum | solution.py:39
  173.9 0.3 fusion.45
  174.4 39.5 %all-reduce.4 = (f32[4]{0:T(128)S(1)}, f32[4,8]{1,0:T(4,128)S(1)}) all-reduce(f32[4]{0:T(128)S(1)} %reduce_sum.212, f32[4,8]{1,0:T(4,128)S(1)} %reduce_sum.213), channel_id=1, replica_groups=mesh['group'=4,'expert'=8] {'group','expert'}, use_global_device_ids=true, to_apply=%region_5.5 | all-reduce | flops 36 | bytes 288 | tf_op jit(solution)/shard_map/while/body/eval_jaxpr/psum | solution.py:39
  214.2 0.3 fusion.45
  214.7 40.5 %all-reduce.4 = (f32[4]{0:T(128)S(1)}, f32[4,8]{1,0:T(4,128)S(1)}) all-reduce(f32[4]{0:T(128)S(1)} %reduce_sum.212, f32[4,8]{1,0:T(4,128)S(1)} %reduce_sum.213), channel_id=1, replica_groups=mesh['group'=4,'expert'=8] {'group','expert'}, use_global_device_ids=true, to_apply=%region_5.5 | all-reduce | flops 36 | bytes 288 | tf_op jit(solution)/shard_map/while/body/eval_jaxpr/psum | solution.py:39
  255.4 0.3 fusion.45
  256.0 39.4 %all-reduce.4 = (f32[4]{0:T(128)S(1)}, f32[4,8]{1,0:T(4,128)S(1)}) all-reduce(f32[4]{0:T(128)S(1)} %reduce_sum.212, f32[4,8]{1,0:T(4,128)S(1)} %reduce_sum.213), channel_id=1, replica_groups=mesh['group'=4,'expert'=8] {'group','expert'}, use_global_device_ids=true, to_apply=%region_5.5 | all-reduce | flops 36 | bytes 288 | tf_op jit(solution)/shard_map/while/body/eval_jaxpr/psum | solution.py:39
  295.6 0.3 fusion.45
  296.1 40.6 %all-reduce.4 = (f32[4]{0:T(128)S(1)}, f32[4,8]{1,0:T(4,128)S(1)}) all-reduce(f32[4]{0:T(128)S(1)} %reduce_sum.212, f32[4,8]{1,0:T(4,128)S(1)} %reduce_sum.213), channel_id=1, replica_groups=mesh['group'=4,'expert'=8] {'group','expert'}, use_global_device_ids=true, to_apply=%region_5.5 | all-reduce | flops 36 | bytes 288 | tf_op jit(solution)/shard_map/while/body/eval_jaxpr/psum | solution.py:39
  336.9 0.3 fusion.45
  337.3 2.4 gather_fusion.2
  339.7 0.1 reshape.224
  340.0 0.1 reshape.227
  340.1 2.0 gather_fusion.3
  342.3 8.4 %fusion.17 = (f32[512]{0:T(512)S(1)}, f32[512,1024]{1,0:T(8,128)S(1)}) fusion(bf16[1,512,1024]{2,1,0:T(8,128)(2,1)} %param.14, bf16[512,3584]{1,0:T(8,128)(2,1)} %bitcast.18, bf16[1,1024,3584]{2,1,0:T(8,128)(2,1)} %param.15), kind=kOutput, calls=%fused_computation.49 | convolution fusion | flops 3759668736 | bytes 14157824 | tf_op jit(solution)/shard_map/dot_general | solution.py:126
  350.8 0.7 reshape.275
  351.5 3.4 all-to-all-start.4
  354.9 5.5 all-to-all-done.4
  360.4 0.5 broadcast.296
  360.9 0.7 reduce.2
  361.6 0.6 copy.115
  362.2 4.6 all-to-all-start.5
  366.9 4.7 all-to-all-done.5
  371.7 2.0 gather_fusion.1
  373.9 204.3 %while.37 = (s32[]{:T(128)}, f32[128,4]{0,1:T(4,128)S(1)}, f32[128,4,8]{0,2,1:T(8,128)S(1)}, f32[5,4]{1,0:T(8,128)S(1)}, f32[5,128,4]{1,2,0:T(4,128)S(1)}, /*ind...) while((s32[]{:T(128)}, f32[128,4]{0,1:T(4,128)S(1)}, ...), condition=%wide.region_28.29_spmd, body=%wide.region_19.28_spmd.sunk | while | flops 52050 | bytes 159945 | solution.py:157
  374.1 0.6 fusion.50
  375.0 38.3 %all-reduce.5 = (f32[4]{0:T(128)S(1)}, f32[4,8]{1,0:T(4,128)S(1)}) all-reduce(f32[4]{0:T(128)S(1)} %fusion.48, f32[4,8]{1,0:T(4,128)S(1)} %get-tuple-element.338), channel_id=1, replica_groups=mesh['group'=4,'expert'=8] {'group','expert'}, use_global_device_ids=true, to_apply=%region_23.23 | all-reduce | flops 36 | bytes 288 | tf_op jit(solution)/shard_map/while/body/eval_jaxpr/psum | solution.py:56
  413.5 0.6 fusion.50
  414.5 40.1 %all-reduce.5 = (f32[4]{0:T(128)S(1)}, f32[4,8]{1,0:T(4,128)S(1)}) all-reduce(f32[4]{0:T(128)S(1)} %fusion.48, f32[4,8]{1,0:T(4,128)S(1)} %get-tuple-element.338), channel_id=1, replica_groups=mesh['group'=4,'expert'=8] {'group','expert'}, use_global_device_ids=true, to_apply=%region_23.23 | all-reduce | flops 36 | bytes 288 | tf_op jit(solution)/shard_map/while/body/eval_jaxpr/psum | solution.py:56
  454.9 0.6 fusion.50
  455.8 39.9 %all-reduce.5 = (f32[4]{0:T(128)S(1)}, f32[4,8]{1,0:T(4,128)S(1)}) all-reduce(f32[4]{0:T(128)S(1)} %fusion.48, f32[4,8]{1,0:T(4,128)S(1)} %get-tuple-element.338), channel_id=1, replica_groups=mesh['group'=4,'expert'=8] {'group','expert'}, use_global_device_ids=true, to_apply=%region_23.23 | all-reduce | flops 36 | bytes 288 | tf_op jit(solution)/shard_map/while/body/eval_jaxpr/psum | solution.py:56
  496.0 0.6 fusion.50
  496.9 40.1 %all-reduce.5 = (f32[4]{0:T(128)S(1)}, f32[4,8]{1,0:T(4,128)S(1)}) all-reduce(f32[4]{0:T(128)S(1)} %fusion.48, f32[4,8]{1,0:T(4,128)S(1)} %get-tuple-element.338), channel_id=1, replica_groups=mesh['group'=4,'expert'=8] {'group','expert'}, use_global_device_ids=true, to_apply=%region_23.23 | all-reduce | flops 36 | bytes 288 | tf_op jit(solution)/shard_map/while/body/eval_jaxpr/psum | solution.py:56
  537.3 0.6 fusion.50
  538.3 39.8 %all-reduce.5 = (f32[4]{0:T(128)S(1)}, f32[4,8]{1,0:T(4,128)S(1)}) all-reduce(f32[4]{0:T(128)S(1)} %fusion.48, f32[4,8]{1,0:T(4,128)S(1)} %get-tuple-element.338), channel_id=1, replica_groups=mesh['group'=4,'expert'=8] {'group','expert'}, use_global_device_ids=true, to_apply=%region_23.23 | all-reduce | flops 36 | bytes 288 | tf_op jit(solution)/shard_map/while/body/eval_jaxpr/psum | solution.py:56
  578.3 0.1 copy.108
  578.4 0.2 reshape.237
  578.6 2.2 scatter_custom_fusion
  580.8 0.6 copy.109
  581.5 3.6 all-to-all-start
  585.0 0.6 bitcast_multiply_fusion.4
  585.6 4.1 all-to-all-done
  589.7 0.6 copy.110
  590.3 3.2 all-to-all-start.1
  593.6 0.6 subtract_multiply_fusion.2
  594.2 5.0 all-to-all-done.1
  599.2 1.2 fusion.18
  (156 shorter events, 6.7 us)
Async XLA Ops:
  0.6 6.1 %copy-start = (bf16[128,3584]{1,0:T(8,128)(2,1)S(1)}, bf16[128,3584]{1,0:T(8,128)(2,1)}, u32[]{:S(2)}) copy-start(bf16[128,3584]{1,0:T(8,128)(2,1)} %param.13) | copy-start | bytes 2752516
  14.6 5.4 copy-start.2
  14.6 5.7 copy-start.3
  14.6 5.7 copy-start.1
  14.6 48.9 %all-to-all-start.2 = ((bf16[4,8,16,3584]{3,2,0,1:T(8,128)(2,1)}), bf16[4,8,16,3584]{3,2,0,1:T(8,128)(2,1)}, u32[]{:S(2)}, u32[]{:S(2)}) async-start(bf16[4,8,16,3584]{3,2,0,1:T(8,128)(2,1)} %fusion.16), calls=%async_computation.2 | async-start | bytes 7340032 | tf_op jit(solution)/shard_map/all_to_all | solution.py:64
  67.6 274.7 %all-to-all-start.3 = ((bf16[4,8,16,3584]{3,2,1,0:T(8,128)(2,1)}), bf16[4,8,16,3584]{3,2,1,0:T(8,128)(2,1)}, u32[]{:S(2)}, u32[]{:S(2)}) async-start(bf16[4,8,16,3584]{3,2,1,0:T(8,128)(2,1)} %copy.114), calls=%async_computation.3 | async-start | bytes 7340032 | tf_op jit(solution)/shard_map/all_to_all | solution.py:68
  351.5 8.9 %all-to-all-start.4 = ((f32[4,1,128]{2,1,0:T(1,128)}), f32[4,1,128]{2,1,0:T(1,128)S(1)}, u32[]{:S(2)}, u32[]{:S(2)}) async-start(f32[4,1,128]{2,1,0:T(1,128)} %reshape.275), calls=%async_computation.4 | async-start | bytes 4096 | tf_op jit(solution)/shard_map/all_to_all | solution.py:133
  362.2 9.4 %all-to-all-start.5 = ((f32[4,8,16]{2,0,1:T(4,128)}), f32[4,8,16]{2,0,1:T(4,128)S(1)}, u32[]{:S(2)}, u32[]{:S(2)}) async-start(f32[4,8,16]{2,0,1:T(4,128)} %copy.115), calls=%async_computation.5 | async-start | bytes 32768 | tf_op jit(solution)/shard_map/all_to_all | solution.py:132
  581.5 8.3 %all-to-all-start = ((bf16[4,8,16]{2,0,1:T(4,128)(2,1)}), bf16[4,8,16]{2,0,1:T(4,128)(2,1)S(1)}, u32[]{:S(2)}, u32[]{:S(2)}) async-start(bf16[4,8,16]{2,0,1:T(4,128)(2,1)} %copy.109), calls=%async_computation | async-start | bytes 16384 | tf_op jit(solution)/shard_map/all_to_all | solution.py:65
  590.3 8.8 %all-to-all-start.1 = ((bf16[4,8,16]{2,1,0:T(8,128)(2,1)}), bf16[4,8,16]{2,1,0:T(8,128)(2,1)S(1)}, u32[]{:S(2)}, u32[]{:S(2)}) async-start(bf16[4,8,16]{2,1,0:T(8,128)(2,1)} %copy.110), calls=%async_computation.1 | async-start | bytes 16384 | tf_op jit(solution)/shard_map/all_to_all | solution.py:69
where the time goes:
time: 602 us; the launch traced here: 600 us
  blocking collectives  458 us (76%)
  waiting for transfers between devices  62.5 us (10%)
  local copies, waits for them, and re-layouts  26.5 us (4%)
  starting transfers between devices  25.7 us (4%)
  other arithmetic  17.9 us (3%)
  matrix products  8.44 us (1%)
    psum x5, blocking collectives, balance_step(): lax.psum((jnp.sum(group_in, 0), jnp.sum(expert_in, 0)), ('group', 'expert'))  260 us
    psum x5, blocking collectives, adjoint_step(): inner_g, inner_e = lax.psum((inner_g, inner_e), ('group', 'expert'))  198 us
    all_to_all x1, waiting for transfers between devices, deliver(): lax.all_to_all(payload[0], 'expert', split_axis=1, concat_axis=1, tiled=T...  43.2 us
  transfers between devices with their start and end apart: 6, of which 5 were waited for; matrix products, arithmetic and copies ran while one was open for 2% of the time, Pallas kernels for 0%

commit v1 on v0

--- a/solution.py
+++ b/solution.py
@@ -36,9 +36,13 @@
 def balance_step(targets, current, unused):
     target_group, target_expert = targets
     group_in, expert_in = current
-    group_cols, expert_cols = lax.psum(
-        (jnp.sum(group_in, 0), jnp.sum(expert_in, 0)), ("group", "expert")
-    )
+
+    def build_views_on(xin):
+        for nth in ("expert", "group"):
+            xin = lax.psum(xin, axis_name=nth)
+        return xin
+
+    group_cols, expert_cols = build_views_on((jnp.sum(group_in, 0), jnp.sum(expert_in, 0)))
     scaled_g, rowsum_g = balance_level(group_in, target_group, group_cols)
     scaled_e, rowsum_e = balance_level(expert_in, target_expert, expert_cols)
     return (

time: 602 us -> 507 us (0.84)
  blocking collectives: 458 us -> 364 us
    psum x5 -> x10, blocking collectives: 260 us -> 166 us  [build_views_on(): xin = lax.psum(xin, axis_name=nth)]
where the time goes in v1:
time: 507 us; the launch traced here: 505 us
  blocking collectives  364 us (72%)
  waiting for transfers between devices  62.2 us (12%)
  local copies, waits for them, and re-layouts  26.4 us (5%)
  starting transfers between devices  24.5 us (5%)
  other arithmetic  17.9 us (4%)
  matrix products  8.44 us (2%)
    psum x5, blocking collectives, adjoint_step(): inner_g, inner_e = lax.psum((inner_g, inner_e), ('group', 'expert'))  198 us
    psum x10, blocking collectives, build_views_on(): xin = lax.psum(xin, axis_name=nth)  166 us
    all_to_all x1, waiting for transfers between devices, deliver(): lax.all_to_all(payload[0], 'expert', split_axis=1, concat_axis=1, tiled=T...  43.2 us
  transfers between devices with their start and end apart: 6, of which 5 were waited for; matrix products, arithmetic and copies ran while one was open for 2% of the time, Pallas kernels for 0%

profile of v1, /device:TPU:0, one launch (start us, length us, event | category | flops | bytes accessed | tf_op | source)
XLA Modules:
  0.0 505.0 jit_solution(6844061879830313497)
XLA Ops:
  0.6 0.9 copy.101
  1.8 0.7 broadcast_multiply_fusion
  2.5 0.6 reduce-window.6
  3.1 0.2 slice_reduce_fusion
  3.4 0.1 mul.222
  3.7 1.4 scatter_custom_fusion.2
  5.2 1.4 scatter_custom_fusion.1
  6.8 4.2 gather_fusion
  10.9 3.6 fusion.16
  14.6 5.3 %all-to-all-start.2 = ((bf16[4,8,16,3584]{3,2,0,1:T(8,128)(2,1)}), bf16[4,8,16,3584]{3,2,0,1:T(8,128)(2,1)}, u32[]{:S(2)}, u32[]{:S(2)}) async-start(bf16[4,8,16,3584]{3,2,0,1:T(8,128)(2,1)} %fusion.16), calls=%async_computation.2 | async-start | bytes 7340032 | tf_op jit(solution)/shard_map/all_to_all | solution.py:68
  20.3 43.2 %all-to-all-done.2 = bf16[4,8,16,3584]{3,2,0,1:T(8,128)(2,1)} async-done(((bf16[4,8,16,3584]{3,2,0,1:T(8,128)(2,1)}), bf16[4,8,16,3584]{3,2,0,1:T(8,128)(2,1)}, u32[]{:S(2)}, u32[]{:S(2)}) %all-to-all-start.2) | async-done | bytes 3670048 | tf_op jit(solution)/shard_map/all_to_all | solution.py:68
  63.5 4.2 copy.114
  67.6 5.6 %all-to-all-start.3 = ((bf16[4,8,16,3584]{3,2,1,0:T(8,128)(2,1)}), bf16[4,8,16,3584]{3,2,1,0:T(8,128)(2,1)}, u32[]{:S(2)}, u32[]{:S(2)}) async-start(bf16[4,8,16,3584]{3,2,1,0:T(8,128)(2,1)} %copy.114), calls=%async_computation.3 | async-start | bytes 7340032 | tf_op jit(solution)/shard_map/all_to_all | solution.py:72
  73.2 170.2 %while.36 = (s32[]{:T(128)}, f32[128,4]{0,1:T(4,128)S(1)}, f32[128,4,8]{0,2,1:T(8,128)S(1)}, f32[5,128,4]{1,2,0:T(4,128)S(1)}, f32[5,128,4,8]{1,3,2,0:T(8,128)S(...) while((s32[]{:T(128)}, f32[128,4]{0,1:T(4,128)S(1)}, ...), condition=%wide.region_12.13_spmd, body=%wide.region_3.12_spmd.sunk | while | flops 15313 | bytes 133421 | solution.py:99
  73.4 12.2 %all-reduce.6 = (f32[4]{0:T(128)S(1)}, f32[4,8]{1,0:T(4,128)S(1)}) all-reduce(f32[4]{0:T(128)S(1)} %reduce_sum.212, f32[4,8]{1,0:T(4,128)S(1)} %reduce_sum.213), channel_id=1, replica_groups=mesh['group'=4,'expert'=8] {'expert'}, use_global_device_ids=true, to_apply=%region_5.5 | all-reduce | flops 36 | bytes 288 | tf_op jit(solution)/shard_map/while/body/eval_jaxpr/psum | solution.py:42
  85.6 50.0 %all-reduce.7 = (f32[4]{0:T(128)S(1)}, f32[4,8]{1,0:T(4,128)S(1)}) all-reduce(f32[4]{0:T(128)S(1)} %get-tuple-element.333, f32[4,8]{1,0:T(4,128)S(1)} %get-tuple-element.334), channel_id=1, replica_groups=mesh['group'=4,'expert'=8] {'group'}, use_global_device_ids=true, to_apply=%region_6.6 | all-reduce | flops 36 | bytes 288 | tf_op jit(solution)/shard_map/while/body/eval_jaxpr/psum | solution.py:42
  135.8 0.3 fusion.45
  136.4 13.4 %all-reduce.6 = (f32[4]{0:T(128)S(1)}, f32[4,8]{1,0:T(4,128)S(1)}) all-reduce(f32[4]{0:T(128)S(1)} %reduce_sum.212, f32[4,8]{1,0:T(4,128)S(1)} %reduce_sum.213), channel_id=1, replica_groups=mesh['group'=4,'expert'=8] {'expert'}, use_global_device_ids=true, to_apply=%region_5.5 | all-reduce | flops 36 | bytes 288 | tf_op jit(solution)/shard_map/while/body/eval_jaxpr/psum | solution.py:42
  149.8 28.2 %all-reduce.7 = (f32[4]{0:T(128)S(1)}, f32[4,8]{1,0:T(4,128)S(1)}) all-reduce(f32[4]{0:T(128)S(1)} %get-tuple-element.333, f32[4,8]{1,0:T(4,128)S(1)} %get-tuple-element.334), channel_id=1, replica_groups=mesh['group'=4,'expert'=8] {'group'}, use_global_device_ids=true, to_apply=%region_6.6 | all-reduce | flops 36 | bytes 288 | tf_op jit(solution)/shard_map/while/body/eval_jaxpr/psum | solution.py:42
  178.2 0.3 fusion.45
  178.8 11.8 %all-reduce.6 = (f32[4]{0:T(128)S(1)}, f32[4,8]{1,0:T(4,128)S(1)}) all-reduce(f32[4]{0:T(128)S(1)} %reduce_sum.212, f32[4,8]{1,0:T(4,128)S(1)} %reduce_sum.213), channel_id=1, replica_groups=mesh['group'=4,'expert'=8] {'expert'}, use_global_device_ids=true, to_apply=%region_5.5 | all-reduce | flops 36 | bytes 288 | tf_op jit(solution)/shard_map/while/body/eval_jaxpr/psum | solution.py:42
  190.6 8.4 %all-reduce.7 = (f32[4]{0:T(128)S(1)}, f32[4,8]{1,0:T(4,128)S(1)}) all-reduce(f32[4]{0:T(128)S(1)} %get-tuple-element.333, f32[4,8]{1,0:T(4,128)S(1)} %get-tuple-element.334), channel_id=1, replica_groups=mesh['group'=4,'expert'=8] {'group'}, use_global_device_ids=true, to_apply=%region_6.6 | all-reduce | flops 36 | bytes 288 | tf_op jit(solution)/shard_map/while/body/eval_jaxpr/psum | solution.py:42
  199.2 0.3 fusion.45
  199.7 11.8 %all-reduce.6 = (f32[4]{0:T(128)S(1)}, f32[4,8]{1,0:T(4,128)S(1)}) all-reduce(f32[4]{0:T(128)S(1)} %reduce_sum.212, f32[4,8]{1,0:T(4,128)S(1)} %reduce_sum.213), channel_id=1, replica_groups=mesh['group'=4,'expert'=8] {'expert'}, use_global_device_ids=true, to_apply=%region_5.5 | all-reduce | flops 36 | bytes 288 | tf_op jit(solution)/shard_map/while/body/eval_jaxpr/psum | solution.py:42
  211.5 10.4 %all-reduce.7 = (f32[4]{0:T(128)S(1)}, f32[4,8]{1,0:T(4,128)S(1)}) all-reduce(f32[4]{0:T(128)S(1)} %get-tuple-element.333, f32[4,8]{1,0:T(4,128)S(1)} %get-tuple-element.334), channel_id=1, replica_groups=mesh['group'=4,'expert'=8] {'group'}, use_global_device_ids=true, to_apply=%region_6.6 | all-reduce | flops 36 | bytes 288 | tf_op jit(solution)/shard_map/while/body/eval_jaxpr/psum | solution.py:42
  222.1 0.3 fusion.45
  222.7 11.8 %all-reduce.6 = (f32[4]{0:T(128)S(1)}, f32[4,8]{1,0:T(4,128)S(1)}) all-reduce(f32[4]{0:T(128)S(1)} %reduce_sum.212, f32[4,8]{1,0:T(4,128)S(1)} %reduce_sum.213), channel_id=1, replica_groups=mesh['group'=4,'expert'=8] {'expert'}, use_global_device_ids=true, to_apply=%region_5.5 | all-reduce | flops 36 | bytes 288 | tf_op jit(solution)/shard_map/while/body/eval_jaxpr/psum | solution.py:42
  234.5 8.4 %all-reduce.7 = (f32[4]{0:T(128)S(1)}, f32[4,8]{1,0:T(4,128)S(1)}) all-reduce(f32[4]{0:T(128)S(1)} %get-tuple-element.333, f32[4,8]{1,0:T(4,128)S(1)} %get-tuple-element.334), channel_id=1, replica_groups=mesh['group'=4,'expert'=8] {'group'}, use_global_device_ids=true, to_apply=%region_6.6 | all-reduce | flops 36 | bytes 288 | tf_op jit(solution)/shard_map/while/body/eval_jaxpr/psum | solution.py:42
  243.0 0.3 fusion.45
  243.4 2.4 gather_fusion.2
  246.1 0.1 reshape.227
  246.3 2.0 gather_fusion.3
  248.4 8.4 %fusion.17 = (f32[512]{0:T(512)S(1)}, f32[512,1024]{1,0:T(8,128)S(1)}) fusion(bf16[1,512,1024]{2,1,0:T(8,128)(2,1)} %param.14, bf16[512,3584]{1,0:T(8,128)(2,1)} %bitcast.18, bf16[1,1024,3584]{2,1,0:T(8,128)(2,1)} %param.15), kind=kOutput, calls=%fused_computation.49 | convolution fusion | flops 3759668736 | bytes 14157824 | tf_op jit(solution)/shard_map/dot_general | solution.py:130
  257.0 0.7 reshape.275
  257.6 3.3 all-to-all-start.4
  260.9 5.5 %all-to-all-done.4 = f32[4,1,128]{2,1,0:T(1,128)S(1)} async-done(((f32[4,1,128]{2,1,0:T(1,128)}), f32[4,1,128]{2,1,0:T(1,128)S(1)}, u32[]{:S(2)}, u32[]{:S(2)}) %all-to-all-start.4) | async-done | bytes 2080 | tf_op jit(solution)/shard_map/all_to_all | solution.py:137
  266.4 0.5 broadcast.296
  266.9 0.7 reduce.2
  267.7 0.6 copy.115
  268.3 3.5 all-to-all-start.5
  271.8 4.5 all-to-all-done.5
  276.4 1.9 gather_fusion.1
  278.7 204.3 %while.37 = (s32[]{:T(128)}, f32[128,4]{0,1:T(4,128)S(1)}, f32[128,4,8]{0,2,1:T(8,128)S(1)}, f32[5,4]{1,0:T(8,128)S(1)}, f32[5,128,4]{1,2,0:T(4,128)S(1)}, /*ind...) while((s32[]{:T(128)}, f32[128,4]{0,1:T(4,128)S(1)}, ...), condition=%wide.region_30.31_spmd, body=%wide.region_21.30_spmd.sunk | while | flops 52050 | bytes 159945 | solution.py:161
  278.8 0.6 fusion.50
  279.7 38.3 %all-reduce.8 = (f32[4]{0:T(128)S(1)}, f32[4,8]{1,0:T(4,128)S(1)}) all-reduce(f32[4]{0:T(128)S(1)} %fusion.48, f32[4,8]{1,0:T(4,128)S(1)} %get-tuple-element.344), channel_id=1, replica_groups=mesh['group'=4,'expert'=8] {'group','expert'}, use_global_device_ids=true, to_apply=%region_25.25 | all-reduce | flops 36 | bytes 288 | tf_op jit(solution)/shard_map/while/body/eval_jaxpr/psum | solution.py:60
  318.2 0.6 fusion.50
  319.2 40.0 %all-reduce.8 = (f32[4]{0:T(128)S(1)}, f32[4,8]{1,0:T(4,128)S(1)}) all-reduce(f32[4]{0:T(128)S(1)} %fusion.48, f32[4,8]{1,0:T(4,128)S(1)} %get-tuple-element.344), channel_id=1, replica_groups=mesh['group'=4,'expert'=8] {'group','expert'}, use_global_device_ids=true, to_apply=%region_25.25 | all-reduce | flops 36 | bytes 288 | tf_op jit(solution)/shard_map/while/body/eval_jaxpr/psum | solution.py:60
  359.5 0.6 fusion.50
  360.5 39.9 %all-reduce.8 = (f32[4]{0:T(128)S(1)}, f32[4,8]{1,0:T(4,128)S(1)}) all-reduce(f32[4]{0:T(128)S(1)} %fusion.48, f32[4,8]{1,0:T(4,128)S(1)} %get-tuple-element.344), channel_id=1, replica_groups=mesh['group'=4,'expert'=8] {'group','expert'}, use_global_device_ids=true, to_apply=%region_25.25 | all-reduce | flops 36 | bytes 288 | tf_op jit(solution)/shard_map/while/body/eval_jaxpr/psum | solution.py:60
  400.6 0.6 fusion.50
  401.6 40.1 %all-reduce.8 = (f32[4]{0:T(128)S(1)}, f32[4,8]{1,0:T(4,128)S(1)}) all-reduce(f32[4]{0:T(128)S(1)} %fusion.48, f32[4,8]{1,0:T(4,128)S(1)} %get-tuple-element.344), channel_id=1, replica_groups=mesh['group'=4,'expert'=8] {'group','expert'}, use_global_device_ids=true, to_apply=%region_25.25 | all-reduce | flops 36 | bytes 288 | tf_op jit(solution)/shard_map/while/body/eval_jaxpr/psum | solution.py:60
  442.0 0.6 fusion.50
  442.9 39.8 %all-reduce.8 = (f32[4]{0:T(128)S(1)}, f32[4,8]{1,0:T(4,128)S(1)}) all-reduce(f32[4]{0:T(128)S(1)} %fusion.48, f32[4,8]{1,0:T(4,128)S(1)} %get-tuple-element.344), channel_id=1, replica_groups=mesh['group'=4,'expert'=8] {'group','expert'}, use_global_device_ids=true, to_apply=%region_25.25 | all-reduce | flops 36 | bytes 288 | tf_op jit(solution)/shard_map/while/body/eval_jaxpr/psum | solution.py:60
  483.1 0.2 reshape.237
  483.3 2.2 scatter_custom_fusion
  485.5 0.6 copy.109
  486.1 3.6 all-to-all-start
  489.7 0.6 bitcast_multiply_fusion.4
  490.3 4.1 all-to-all-done
  494.4 0.6 copy.110
  495.0 3.2 all-to-all-start.1
  498.2 0.6 subtract_multiply_fusion.2
  498.8 5.0 all-to-all-done.1
  503.9 1.2 fusion.18
  (161 shorter events, 7.5 us)
Async XLA Ops:
  0.6 6.1 %copy-start = (bf16[128,3584]{1,0:T(8,128)(2,1)S(1)}, bf16[128,3584]{1,0:T(8,128)(2,1)}, u32[]{:S(2)}) copy-start(bf16[128,3584]{1,0:T(8,128)(2,1)} %param.13) | copy-start | bytes 2752516
  14.6 5.4 %copy-start.2 = (s32[128,2]{0,1:T(2,128)S(1)}, s32[128,2]{0,1:T(2,128)}, u32[]{:S(2)}) copy-start(s32[128,2]{0,1:T(2,128)} %param.12) | copy-start | bytes 3076
  14.6 5.7 %copy-start.3 = (f32[128,4]{0,1:T(4,128)S(1)}, f32[128,4]{0,1:T(4,128)}, u32[]{:S(2)}) copy-start(f32[128,4]{0,1:T(4,128)} %param.10) | copy-start | bytes 6148
  14.6 5.7 %copy-start.1 = (f32[128,32]{0,1:T(8,128)S(1)}, f32[128,32]{0,1:T(8,128)}, u32[]{:S(2)}) copy-start(f32[128,32]{0,1:T(8,128)} %param.11) | copy-start | bytes 49156
  14.6 48.9 %all-to-all-start.2 = ((bf16[4,8,16,3584]{3,2,0,1:T(8,128)(2,1)}), bf16[4,8,16,3584]{3,2,0,1:T(8,128)(2,1)}, u32[]{:S(2)}, u32[]{:S(2)}) async-start(bf16[4,8,16,3584]{3,2,0,1:T(8,128)(2,1)} %fusion.16), calls=%async_computation.2 | async-start | bytes 7340032 | tf_op jit(solution)/shard_map/all_to_all | solution.py:68
  67.6 180.8 %all-to-all-start.3 = ((bf16[4,8,16,3584]{3,2,1,0:T(8,128)(2,1)}), bf16[4,8,16,3584]{3,2,1,0:T(8,128)(2,1)}, u32[]{:S(2)}, u32[]{:S(2)}) async-start(bf16[4,8,16,3584]{3,2,1,0:T(8,128)(2,1)} %copy.114), calls=%async_computation.3 | async-start | bytes 7340032 | tf_op jit(solution)/shard_map/all_to_all | solution.py:72
  257.6 8.8 %all-to-all-start.4 = ((f32[4,1,128]{2,1,0:T(1,128)}), f32[4,1,128]{2,1,0:T(1,128)S(1)}, u32[]{:S(2)}, u32[]{:S(2)}) async-start(f32[4,1,128]{2,1,0:T(1,128)} %reshape.275), calls=%async_computation.4 | async-start | bytes 4096 | tf_op jit(solution)/shard_map/all_to_all | solution.py:137
  268.3 8.0 %all-to-all-start.5 = ((f32[4,8,16]{2,0,1:T(4,128)}), f32[4,8,16]{2,0,1:T(4,128)S(1)}, u32[]{:S(2)}, u32[]{:S(2)}) async-start(f32[4,8,16]{2,0,1:T(4,128)} %copy.115), calls=%async_computation.5 | async-start | bytes 32768 | tf_op jit(solution)/shard_map/all_to_all | solution.py:136
  486.1 8.3 %all-to-all-start = ((bf16[4,8,16]{2,0,1:T(4,128)(2,1)}), bf16[4,8,16]{2,0,1:T(4,128)(2,1)S(1)}, u32[]{:S(2)}, u32[]{:S(2)}) async-start(bf16[4,8,16]{2,0,1:T(4,128)(2,1)} %copy.109), calls=%async_computation | async-start | bytes 16384 | tf_op jit(solution)/shard_map/all_to_all | solution.py:69
  495.0 8.8 %all-to-all-start.1 = ((bf16[4,8,16]{2,1,0:T(8,128)(2,1)}), bf16[4,8,16]{2,1,0:T(8,128)(2,1)S(1)}, u32[]{:S(2)}, u32[]{:S(2)}) async-start(bf16[4,8,16]{2,1,0:T(8,128)(2,1)} %copy.110), calls=%async_computation.1 | async-start | bytes 16384 | tf_op jit(solution)/shard_map/all_to_all | solution.py:73
